TPU v7x, 512 devices: a whole 4x4x16 slice. The times are simulated.
512 devices in a mesh: gy: 16 (over z), gx: 32 (over x, y, core).
Axes of the slice: x: 4, y: 4, z: 16, core: 2. Of those that a mesh axis runs over, the one named last changes fastest.
Arguments:
- observed: float32 [16, 512, 4096], P(None, 'gy', 'gx'), may hold values from 0 to 20, as said below
- profiles: float32 [64, 3, 9], replicated, may hold values from 0.03 to 0.25
- tile_index: int32 [16, 32], replicated, may hold values from 0 to 63
Outputs:
- estimate: float32 [16, 512, 4096], P(None, 'gy', 'gx')
Inputs may be any that keep to these rules, and one draw needn't show every extreme that they name: `observed`: nonnegative intensities.
All inputs are finite; a program needn't handle non-finite values.
Results may differ from a plain program's by a relative error of at most 0.0003.
Values sent between devices are 32-bit elements; how exact they have to be, the bound alone decides.
A program may use at most 64 MiB of HBM per device.

v0:
```python
import jax
import jax.numpy as jnp
from jax import lax
from jax.sharding import PartitionSpec as P

ITERS = 2
WEIGHT_TV = 0.02
SMOOTHING = 0.1
DAMPING = 0.05
START_STEP = 0.5
EXACT_MODE = lax.Precision.HIGHEST


def extended(block, sides, width):
    for axis, dim in sides:
        count = lax.axis_size(axis)
        forward = [(i, i + 1) for i in range(count - 1)]
        backward = [(target, source) for source, target in forward]
        low = lax.ppermute(
            lax.slice_in_dim(block, block.shape[dim] - width, None, axis=dim), axis, forward
        )
        high = lax.ppermute(lax.slice_in_dim(block, 0, width, axis=dim), axis, backward)
        block = jnp.concatenate([low, block, high], axis=dim)
    return block


def from_behind(block, axis, distance):
    devices = range(lax.axis_size(axis))
    route = [(i - distance, i) for i in devices if i - distance in devices]
    return lax.ppermute(block, axis, route)


def band_matrix(profile, source_start, source_len, target_start, target_len, transposed):
    radius = (profile.shape[0] - 1) // 2
    source = jnp.arange(source_len)[:, None] + source_start
    target = jnp.arange(target_len)[None, :] + target_start
    distance = source - target if transposed else target - source
    offsets = jnp.arange(profile.shape[0]) - radius
    return jnp.sum(jnp.where(distance[:, :, None] == offsets, profile, 0.0), axis=2)


def apply_kernel(
    region, kernel, row_start, col_start, out_rows, out_cols, row_target, col_target, transposed
):
    layers, height, breadth = region.shape
    mix_cols = band_matrix(kernel[2], col_start, breadth, col_target, out_cols, transposed)
    along_cols = jnp.dot(
        region.reshape(layers * height, breadth), mix_cols, precision=EXACT_MODE
    ).reshape(layers, height, out_cols)
    mix_rows = band_matrix(kernel[1], row_start, height, row_target, out_rows, transposed)
    along_rows = jnp.einsum("zyx,yo->zox", along_cols, mix_rows, precision=EXACT_MODE)
    mix_depth = band_matrix(kernel[0], 0, layers, 0, layers, transposed)
    return jnp.einsum("zyx,zo->oyx", along_rows, mix_depth, precision=EXACT_MODE)


def pick_kernel(profiles, tile_index, row_pick, col_pick):
    grid_rows, grid_cols = tile_index.shape
    chosen_tile = (jnp.arange(grid_rows)[:, None] == row_pick) & (
        jnp.arange(grid_cols)[None, :] == col_pick
    )
    kernel_number = jnp.sum(jnp.where(chosen_tile, tile_index, 0))
    chosen_kernel = jnp.arange(profiles.shape[0])[:, None, None] == kernel_number
    return jnp.sum(jnp.where(chosen_kernel, profiles, 0.0), axis=0)


def variation_slope(padded, radius, first_row, first_col, total_rows, total_cols):
    height = padded.shape[1] - 2 * radius
    breadth = padded.shape[2] - 2 * radius
    window = padded[:, radius - 1 : radius + height + 1, radius - 1 : radius + breadth + 1]
    core = window[:, : height + 1, : breadth + 1]
    diff_rows = (window[:, 1:, :] - window[:, :-1, :])[:, :, : breadth + 1]
    diff_cols = (window[:, :, 1:] - window[:, :, :-1])[:, : height + 1, :]
    diff_depth = jnp.concatenate([core[1:] - core[:-1], jnp.zeros_like(core[:1])], 0)
    global_rows = first_row - 1 + jnp.arange(height + 1)
    global_cols = first_col - 1 + jnp.arange(breadth + 1)
    diff_rows = jnp.where((global_rows == total_rows - 1)[:, None], 0.0, diff_rows)
    diff_cols = jnp.where((global_cols == total_cols - 1)[None, :], 0.0, diff_cols)
    magnitude = jnp.sqrt(
        diff_depth * diff_depth
        + diff_rows * diff_rows
        + diff_cols * diff_cols
        + SMOOTHING * SMOOTHING
    )
    inside = (global_rows >= 0)[:, None] & (global_cols >= 0)[None, :]
    flux_rows = jnp.where(inside, diff_rows / magnitude, 0.0)
    flux_cols = jnp.where(inside, diff_cols / magnitude, 0.0)
    flux_depth = jnp.where(inside, diff_depth / magnitude, 0.0)[:, 1:, 1:]
    result = flux_rows[:, :-1, 1:] - flux_rows[:, 1:, 1:]
    result = result + flux_cols[:, 1:, :-1] - flux_cols[:, 1:, 1:]
    depth_before = jnp.concatenate([jnp.zeros_like(flux_depth[:1]), flux_depth[:-1]], 0)
    return result + depth_before - flux_depth


def per_device(observed, profiles, tile_index):
    layers, height, breadth = observed.shape
    radius = (profiles.shape[2] - 1) // 2
    row_number = lax.axis_index("gy")
    col_number = lax.axis_index("gx")
    first_row = row_number * height
    first_col = col_number * breadth
    total_rows = lax.axis_size("gy") * height
    total_cols = lax.axis_size("gx") * breadth
    kernel = pick_kernel(profiles, tile_index, row_number, col_number)

    def slope_at(estimate):
        padded = extended(estimate, (("gy", 1), ("gx", 2)), radius)
        blurred = apply_kernel(padded, kernel, 0, 0, height, breadth, radius, radius, False)
        residual = blurred - observed
        spread = apply_kernel(
            residual, kernel, radius, radius, height + 2 * radius, breadth + 2 * radius, 0, 0, True
        )
        from_right = from_behind(spread[:, :, :radius], "gx", -1)
        from_left = from_behind(spread[:, :, breadth + radius :], "gx", 1)
        middle = spread[:, :, radius : breadth + radius]
        middle = (
            middle.at[:, :, :radius].add(from_left).at[:, :, breadth - radius :].add(from_right)
        )
        from_below = from_behind(middle[:, :radius], "gy", -1)
        from_above = from_behind(middle[:, height + radius :], "gy", 1)
        pulled = (
            middle[:, radius : height + radius]
            .at[:, :radius]
            .add(from_above)
            .at[:, height - radius :]
            .add(from_below)
        )
        smooth = variation_slope(padded, radius, first_row, first_col, total_rows, total_cols)
        return pulled + WEIGHT_TV * smooth + DAMPING * estimate

    previous = observed
    prev_descent = slope_at(previous)
    current = previous - START_STEP * prev_descent
    for iteration in range(ITERS):
        descent = slope_at(current)
        change = current - previous
        growth = descent - prev_descent
        change_sq, change_growth = lax.psum(
            (jnp.sum(change * change), jnp.sum(change * growth)), ("gy", "gx")
        )
        step_size = change_sq / change_growth
        previous, prev_descent = (current, descent)
        current = current - step_size * descent
    return current


def solution(mesh):
    in_specs = (P(None, "gy", "gx"), P(), P())
    out_specs = P(None, "gy", "gx")
    return jax.shard_map(
        per_device, mesh=mesh, in_specs=in_specs, out_specs=out_specs, check_vma=False
    )
```

profile of v0, /device:TPU:1, one launch (start us, length us, event | category | flops | bytes accessed | tf_op | source)
XLA Modules:
  0.0 398.4 jit_solution(11025380353578500066)
XLA Ops:
  0.9 4.4 %collective-permute-start = (f32[16,4,128]{2,1,0:T(4,128)S(1)}, f32[16,4,128]{2,1,0:T(4,128)S(1)}, u32[]{:S(2)}, u32[]{:S(2)}) collective-permute-start(f32[16,4,128]{2,1,0:T(4,128)S(1)} %get-tuple-element.209), channel_id=1, source_target_pairs={{0,32},{32,64},{64,96},{96,128},{128,160},{160,192},{192,224},{224... | collective-permute-start | bytes 98312 | tf_op jit(solution)/shard_map/ppermute | solution.py:19
  10.3 5.0 %collective-permute-start.2 = (f32[16,40,4]{2,1,0:T(8,128)S(1)}, f32[16,40,4]{2,1,0:T(8,128)S(1)}, u32[]{:S(2)}, u32[]{:S(2)}) collective-permute-start(f32[16,40,4]{2,1,0:T(8,128)S(1)} %get-tuple-element.203), channel_id=1, source_target_pairs={{0,1},{1,2},{2,3},{3,4},{4,5},{5,6},{6,7},{7,8},{8,9},{9,10},{10,1... | collective-permute-start | bytes 30728 | tf_op jit(solution)/shard_map/ppermute | solution.py:19
  15.4 2.9 collective-permute-start.3
  20.3 3.6 collective-permute-done.3
  36.5 3.6 scatter-add.40
  42.2 5.7 %scatter-add.41 = f32[16,40,128]{2,1,0:T(8,128)S(1)} dynamic-update-slice(f32[16,40,128]{2,1,0:T(8,128)S(1)} %scatter-add.40, f32[16,40,4]{2,1,0:T(8,128)} %slice_add_fusion.2, s32[]{:T(128)} %constant.298.clone.1, s32[]{:T(128)} %constant.298.clone.1, s32[]{:T(128)} %constant.301.clone.1) | dynamic-update-slice | bytes 20484 | tf_op jit(solution)/shard_map/scatter-add | solution.py:116
  47.9 3.5 collective-permute-start.6
  53.3 4.6 %collective-permute-done.7 = f32[16,4,128]{2,1,0:T(4,128)S(1)} collective-permute-done((f32[16,4,128]{2,1,0:T(4,128)S(1)}, f32[16,4,128]{2,1,0:T(4,128)S(1)}, u32[]{:S(2)}, u32[]{:S(2)}) %collective-permute-start.7) | collective-permute-done | bytes 32800 | tf_op jit(solution)/shard_map/ppermute | solution.py:30
  59.1 4.8 %collective-permute-start.8 = (f32[16,4,128]{2,1,0:T(4,128)S(1)}, f32[16,4,128]{2,1,0:T(4,128)S(1)}, u32[]{:S(2)}, u32[]{:S(2)}) collective-permute-start(f32[16,4,128]{2,1,0:T(4,128)S(1)} %get-tuple-element.207), channel_id=1, source_target_pairs={{0,32},{32,64},{64,96},{96,128},{128,160},{160,192},{192,224},{224... | collective-permute-start | bytes 98312 | tf_op jit(solution)/shard_map/ppermute | solution.py:19
  65.2 3.4 collective-permute-done.9
  68.8 6.7 %collective-permute-start.10 = (f32[16,40,4]{2,1,0:T(8,128)S(1)}, f32[16,40,4]{2,1,0:T(8,128)S(1)}, u32[]{:S(2)}, u32[]{:S(2)}) collective-permute-start(f32[16,40,4]{2,1,0:T(8,128)S(1)} %get-tuple-element.199), channel_id=1, source_target_pairs={{0,1},{1,2},{2,3},{3,4},{4,5},{5,6},{6,7},{7,8},{8,9},{9,10},{10,1... | collective-permute-start | bytes 30728 | tf_op jit(solution)/shard_map/ppermute | solution.py:19
  80.5 3.4 collective-permute-done.11
  97.6 3.5 scatter-add.46
  102.7 5.7 %scatter-add.49 = f32[16,40,128]{2,1,0:T(8,128)S(1)} dynamic-update-slice(f32[16,40,128]{2,1,0:T(8,128)S(1)} %scatter-add.46, f32[16,40,4]{2,1,0:T(8,128)S(1)} %slice_add_fusion.1, s32[]{:T(128)} %constant.298.clone.1, s32[]{:T(128)} %constant.298.clone.1, s32[]{:T(128)} %constant.301.clone.1) | dynamic-update-slice | bytes 20484 | tf_op jit(solution)/shard_map/scatter-add | solution.py:116
  108.4 4.1 %collective-permute-start.14 = (f32[16,4,128]{2,1,0:T(4,128)S(1)}, f32[16,4,128]{2,1,0:T(4,128)S(1)}, u32[]{:S(2)}, u32[]{:S(2)}) collective-permute-start(f32[16,4,128]{2,1,0:T(4,128)S(1)} %get-tuple-element.198), channel_id=1, source_target_pairs={{0,32},{32,64},{64,96},{96,128},{128,160},{160,192},{192,224},{224... | collective-permute-start | bytes 98312 | tf_op jit(solution)/shard_map/ppermute | solution.py:30
  114.4 3.6 collective-permute-done.15
  119.2 113.8 %all-reduce.7 = (f32[]{:T(128)}, f32[]{:T(128)}) all-reduce(f32[]{:T(128)} %get-tuple-element.152, f32[]{:T(128)} %get-tuple-element.151), channel_id=1, replica_groups=mesh['gy'=16,'gx'=32] {'gy','gx'}, use_global_device_ids=true, to_apply=%region_9.10 | all-reduce | flops 2 | bytes 16 | tf_op jit(solution)/shard_map/psum | solution.py:137
  236.9 3.3 collective-permute-done.17
  240.5 3.8 collective-permute-start.18
  249.3 3.4 collective-permute-done.19
  267.1 3.6 scatter-add.54
  272.5 5.7 %scatter-add.55 = f32[16,40,128]{2,1,0:T(8,128)S(1)} dynamic-update-slice(f32[16,40,128]{2,1,0:T(8,128)S(1)} %scatter-add.54, f32[16,40,4]{2,1,0:T(8,128)} %slice_add_fusion, s32[]{:T(128)} %constant.298.clone.1, s32[]{:T(128)} %constant.298.clone.1, s32[]{:T(128)} %constant.301.clone.1) | dynamic-update-slice | bytes 20484 | tf_op jit(solution)/shard_map/scatter-add | solution.py:116
  283.1 4.0 collective-permute-done.23
  288.2 108.2 %all-reduce.6 = (f32[]{:T(128)}, f32[]{:T(128)}) all-reduce(f32[]{:T(128)} %get-tuple-element.150, f32[]{:T(128)} %get-tuple-element.149), channel_id=1, replica_groups=mesh['gy'=16,'gx'=32] {'gy','gx'}, use_global_device_ids=true, to_apply=%region_13.14 | all-reduce | flops 2 | bytes 16 | tf_op jit(solution)/shard_map/psum | solution.py:137
  (211 shorter events, 80.2 us)
Async XLA Ops:
  0.9 8.8 %collective-permute-start = (f32[16,4,128]{2,1,0:T(4,128)S(1)}, f32[16,4,128]{2,1,0:T(4,128)S(1)}, u32[]{:S(2)}, u32[]{:S(2)}) collective-permute-start(f32[16,4,128]{2,1,0:T(4,128)S(1)} %get-tuple-element.209), channel_id=1, source_target_pairs={{0,32},{32,64},{64,96},{96,128},{128,160},{160,192},{192,224},{224... | collective-permute-start | bytes 98312 | tf_op jit(solution)/shard_map/ppermute | solution.py:19
  5.3 4.8 %collective-permute-start.1 = (f32[16,4,128]{2,1,0:T(4,128)S(1)}, f32[16,4,128]{2,1,0:T(4,128)S(1)}, u32[]{:S(2)}, u32[]{:S(2)}) collective-permute-start(f32[16,4,128]{2,1,0:T(4,128)S(1)} %get-tuple-element.210), channel_id=1, source_target_pairs={{32,0},{64,32},{96,64},{128,96},{160,128},{192,160},{224,192},{256... | collective-permute-start | bytes 98312 | tf_op jit(solution)/shard_map/ppermute | solution.py:22
  10.3 9.0 %collective-permute-start.2 = (f32[16,40,4]{2,1,0:T(8,128)S(1)}, f32[16,40,4]{2,1,0:T(8,128)S(1)}, u32[]{:S(2)}, u32[]{:S(2)}) collective-permute-start(f32[16,40,4]{2,1,0:T(8,128)S(1)} %get-tuple-element.203), channel_id=1, source_target_pairs={{0,1},{1,2},{2,3},{3,4},{4,5},{5,6},{6,7},{7,8},{8,9},{9,10},{10,1... | collective-permute-start | bytes 30728 | tf_op jit(solution)/shard_map/ppermute | solution.py:19
  15.4 8.4 %collective-permute-start.3 = (f32[16,40,4]{2,1,0:T(8,128)S(1)}, f32[16,40,4]{2,1,0:T(8,128)S(1)}, u32[]{:S(2)}, u32[]{:S(2)}) collective-permute-start(f32[16,40,4]{2,1,0:T(8,128)S(1)} %get-tuple-element.204), channel_id=1, source_target_pairs={{1,0},{2,1},{3,2},{4,3},{5,4},{6,5},{7,6},{8,7},{9,8},{10,9},{11,1... | collective-permute-start | bytes 30728 | tf_op jit(solution)/shard_map/ppermute | solution.py:22
  29.7 5.9 %collective-permute-start.4 = (f32[16,40,4]{2,1,0:T(8,128)S(1)}, f32[16,40,4]{2,1,0:T(8,128)S(1)}, u32[]{:S(2)}, u32[]{:S(2)}) collective-permute-start(f32[16,40,4]{2,1,0:T(8,128)S(1)} %copy.86), channel_id=1, source_target_pairs={{0,1},{1,2},{2,3},{3,4},{4,5},{5,6},{6,7},{7,8},{8,9},{9,10},{10,1... | collective-permute-start | bytes 30728 | tf_op jit(solution)/shard_map/ppermute | solution.py:30
  31.6 8.7 %collective-permute-start.5 = (f32[16,40,4]{2,1,0:T(8,128)}, f32[16,40,4]{2,1,0:T(8,128)}, u32[]{:S(2)}, u32[]{:S(2)}) collective-permute-start(f32[16,40,4]{2,1,0:T(8,128)} %copy.87), channel_id=1, source_target_pairs={{1,0},{2,1},{3,2},{4,3},{5,4},{6,5},{7,6},{8,7},{9,8},{10,9},{11,1... | collective-permute-start | bytes 30728 | tf_op jit(solution)/shard_map/ppermute | solution.py:30
  47.9 5.3 %collective-permute-start.6 = (f32[16,4,128]{2,1,0:T(4,128)S(1)}, f32[16,4,128]{2,1,0:T(4,128)S(1)}, u32[]{:S(2)}, u32[]{:S(2)}) collective-permute-start(f32[16,4,128]{2,1,0:T(4,128)S(1)} %get-tuple-element.202), channel_id=1, source_target_pairs={{0,32},{32,64},{64,96},{96,128},{128,160},{160,192},{192,224},{224... | collective-permute-start | bytes 98312 | tf_op jit(solution)/shard_map/ppermute | solution.py:30
  52.0 6.0 %collective-permute-start.7 = (f32[16,4,128]{2,1,0:T(4,128)S(1)}, f32[16,4,128]{2,1,0:T(4,128)S(1)}, u32[]{:S(2)}, u32[]{:S(2)}) collective-permute-start(f32[16,4,128]{2,1,0:T(4,128)S(1)} %get-tuple-element.201), channel_id=1, source_target_pairs={{32,0},{64,32},{96,64},{128,96},{160,128},{192,160},{224,192},{256... | collective-permute-start | bytes 98312 | tf_op jit(solution)/shard_map/ppermute | solution.py:30
  59.1 6.2 %collective-permute-start.8 = (f32[16,4,128]{2,1,0:T(4,128)S(1)}, f32[16,4,128]{2,1,0:T(4,128)S(1)}, u32[]{:S(2)}, u32[]{:S(2)}) collective-permute-start(f32[16,4,128]{2,1,0:T(4,128)S(1)} %get-tuple-element.207), channel_id=1, source_target_pairs={{0,32},{32,64},{64,96},{96,128},{128,160},{160,192},{192,224},{224... | collective-permute-start | bytes 98312 | tf_op jit(solution)/shard_map/ppermute | solution.py:19
  63.9 4.7 %collective-permute-start.9 = (f32[16,4,128]{2,1,0:T(4,128)S(1)}, f32[16,4,128]{2,1,0:T(4,128)S(1)}, u32[]{:S(2)}, u32[]{:S(2)}) collective-permute-start(f32[16,4,128]{2,1,0:T(4,128)S(1)} %get-tuple-element.208), channel_id=1, source_target_pairs={{32,0},{64,32},{96,64},{128,96},{160,128},{192,160},{224,192},{256... | collective-permute-start | bytes 98312 | tf_op jit(solution)/shard_map/ppermute | solution.py:22
  68.8 10.7 %collective-permute-start.10 = (f32[16,40,4]{2,1,0:T(8,128)S(1)}, f32[16,40,4]{2,1,0:T(8,128)S(1)}, u32[]{:S(2)}, u32[]{:S(2)}) collective-permute-start(f32[16,40,4]{2,1,0:T(8,128)S(1)} %get-tuple-element.199), channel_id=1, source_target_pairs={{0,1},{1,2},{2,3},{3,4},{4,5},{5,6},{6,7},{7,8},{8,9},{9,10},{10,1... | collective-permute-start | bytes 30728 | tf_op jit(solution)/shard_map/ppermute | solution.py:19
  75.5 8.4 %collective-permute-start.11 = (f32[16,40,4]{2,1,0:T(8,128)S(1)}, f32[16,40,4]{2,1,0:T(8,128)S(1)}, u32[]{:S(2)}, u32[]{:S(2)}) collective-permute-start(f32[16,40,4]{2,1,0:T(8,128)S(1)} %get-tuple-element.200), channel_id=1, source_target_pairs={{1,0},{2,1},{3,2},{4,3},{5,4},{6,5},{7,6},{8,7},{9,8},{10,9},{11,1... | collective-permute-start | bytes 30728 | tf_op jit(solution)/shard_map/ppermute | solution.py:22
  90.8 6.7 %collective-permute-start.12 = (f32[16,40,4]{2,1,0:T(8,128)S(1)}, f32[16,40,4]{2,1,0:T(8,128)S(1)}, u32[]{:S(2)}, u32[]{:S(2)}) collective-permute-start(f32[16,40,4]{2,1,0:T(8,128)S(1)} %copy.90), channel_id=1, source_target_pairs={{0,1},{1,2},{2,3},{3,4},{4,5},{5,6},{6,7},{7,8},{8,9},{9,10},{10,1... | collective-permute-start | bytes 30728 | tf_op jit(solution)/shard_map/ppermute | solution.py:30
  92.7 8.8 %collective-permute-start.13 = (f32[16,40,4]{2,1,0:T(8,128)}, f32[16,40,4]{2,1,0:T(8,128)}, u32[]{:S(2)}, u32[]{:S(2)}) collective-permute-start(f32[16,40,4]{2,1,0:T(8,128)} %copy.91), channel_id=1, source_target_pairs={{1,0},{2,1},{3,2},{4,3},{5,4},{6,5},{7,6},{8,7},{9,8},{10,9},{11,1... | collective-permute-start | bytes 30728 | tf_op jit(solution)/shard_map/ppermute | solution.py:30
  108.4 6.0 %collective-permute-start.14 = (f32[16,4,128]{2,1,0:T(4,128)S(1)}, f32[16,4,128]{2,1,0:T(4,128)S(1)}, u32[]{:S(2)}, u32[]{:S(2)}) collective-permute-start(f32[16,4,128]{2,1,0:T(4,128)S(1)} %get-tuple-element.198), channel_id=1, source_target_pairs={{0,32},{32,64},{64,96},{96,128},{128,160},{160,192},{192,224},{224... | collective-permute-start | bytes 98312 | tf_op jit(solution)/shard_map/ppermute | solution.py:30
  113.0 5.1 %collective-permute-start.15 = (f32[16,4,128]{2,1,0:T(4,128)S(1)}, f32[16,4,128]{2,1,0:T(4,128)S(1)}, u32[]{:S(2)}, u32[]{:S(2)}) collective-permute-start(f32[16,4,128]{2,1,0:T(4,128)S(1)} %get-tuple-element.197), channel_id=1, source_target_pairs={{32,0},{64,32},{96,64},{128,96},{160,128},{192,160},{224,192},{256... | collective-permute-start | bytes 98312 | tf_op jit(solution)/shard_map/ppermute | solution.py:30
  234.3 2.6 collective-permute-start.16
  235.6 4.7 %collective-permute-start.17 = (f32[16,4,128]{2,1,0:T(4,128)S(1)}, f32[16,4,128]{2,1,0:T(4,128)S(1)}, u32[]{:S(2)}, u32[]{:S(2)}) collective-permute-start(f32[16,4,128]{2,1,0:T(4,128)S(1)} %get-tuple-element.206), channel_id=1, source_target_pairs={{32,0},{64,32},{96,64},{128,96},{160,128},{192,160},{224,192},{256... | collective-permute-start | bytes 98312 | tf_op jit(solution)/shard_map/ppermute | solution.py:22
  240.5 7.8 %collective-permute-start.18 = (f32[16,40,4]{2,1,0:T(8,128)S(1)}, f32[16,40,4]{2,1,0:T(8,128)S(1)}, u32[]{:S(2)}, u32[]{:S(2)}) collective-permute-start(f32[16,40,4]{2,1,0:T(8,128)S(1)} %get-tuple-element.195), channel_id=1, source_target_pairs={{0,1},{1,2},{2,3},{3,4},{4,5},{5,6},{6,7},{7,8},{8,9},{9,10},{10,1... | collective-permute-start | bytes 30728 | tf_op jit(solution)/shard_map/ppermute | solution.py:19
  244.3 8.4 %collective-permute-start.19 = (f32[16,40,4]{2,1,0:T(8,128)S(1)}, f32[16,40,4]{2,1,0:T(8,128)S(1)}, u32[]{:S(2)}, u32[]{:S(2)}) collective-permute-start(f32[16,40,4]{2,1,0:T(8,128)S(1)} %get-tuple-element.196), channel_id=1, source_target_pairs={{1,0},{2,1},{3,2},{4,3},{5,4},{6,5},{7,6},{8,7},{9,8},{10,9},{11,1... | collective-permute-start | bytes 30728 | tf_op jit(solution)/shard_map/ppermute | solution.py:22
  259.5 6.7 %collective-permute-start.20 = (f32[16,40,4]{2,1,0:T(8,128)S(1)}, f32[16,40,4]{2,1,0:T(8,128)S(1)}, u32[]{:S(2)}, u32[]{:S(2)}) collective-permute-start(f32[16,40,4]{2,1,0:T(8,128)S(1)} %copy.94), channel_id=1, source_target_pairs={{0,1},{1,2},{2,3},{3,4},{4,5},{5,6},{6,7},{7,8},{8,9},{9,10},{10,1... | collective-permute-start | bytes 30728 | tf_op jit(solution)/shard_map/ppermute | solution.py:30
  261.4 9.2 %collective-permute-start.21 = (f32[16,40,4]{2,1,0:T(8,128)}, f32[16,40,4]{2,1,0:T(8,128)}, u32[]{:S(2)}, u32[]{:S(2)}) collective-permute-start(f32[16,40,4]{2,1,0:T(8,128)} %copy.95), channel_id=1, source_target_pairs={{1,0},{2,1},{3,2},{4,3},{5,4},{6,5},{7,6},{8,7},{9,8},{10,9},{11,1... | collective-permute-start | bytes 30728 | tf_op jit(solution)/shard_map/ppermute | solution.py:30
  278.3 4.8 %collective-permute-start.22 = (f32[16,4,128]{2,1,0:T(4,128)S(1)}, f32[16,4,128]{2,1,0:T(4,128)S(1)}, u32[]{:S(2)}, u32[]{:S(2)}) collective-permute-start(f32[16,4,128]{2,1,0:T(4,128)S(1)} %get-tuple-element.194), channel_id=1, source_target_pairs={{0,32},{32,64},{64,96},{96,128},{128,160},{160,192},{192,224},{224... | collective-permute-start | bytes 98312 | tf_op jit(solution)/shard_map/ppermute | solution.py:30
  281.6 5.4 %collective-permute-start.23 = (f32[16,4,128]{2,1,0:T(4,128)S(1)}, f32[16,4,128]{2,1,0:T(4,128)S(1)}, u32[]{:S(2)}, u32[]{:S(2)}) collective-permute-start(f32[16,4,128]{2,1,0:T(4,128)S(1)} %get-tuple-element.193), channel_id=1, source_target_pairs={{32,0},{64,32},{96,64},{128,96},{160,128},{192,160},{224,192},{256... | collective-permute-start | bytes 98312 | tf_op jit(solution)/shard_map/ppermute | solution.py:30
  (34 other events, 355.5 us)
where the time goes:
time: 400 us; the launch traced here: 398 us
  blocking collectives  222 us (56%)
  starting transfers between devices  64.8 us (16%)
  local copies, waits for them, and re-layouts  40.1 us (10%)
  waiting for transfers between devices  35.8 us (9%)
  other arithmetic  20.8 us (5%)
  matrix products  11.2 us (3%)
    psum x2, blocking collectives, per_device(): lax.psum((jnp.sum(change * change), jnp.sum(change * growth)), ('gy', 'gx'))  222 us
    scatter-add x6, local copies, waits for them, and re-layouts, slope_at(): middle.at[:, :, :radius].add(from_left).at[:, :, breadth - radius:]  27.7 us
    ppermute x12, starting transfers between devices, from_behind(): return lax.ppermute(block, axis, route)  27.7 us
    ppermute x6, starting transfers between devices, extended(): lax.ppermute(lax.slice_in_dim(block, block.shape[dim] - width, None, axis...  26.1 us
    ppermute x6, waiting for transfers between devices, extended(): lax.ppermute(lax.slice_in_dim(block, 0, width, axis=dim), axis, backward)  17.5 us
    ppermute x12, waiting for transfers between devices, from_behind(): return lax.ppermute(block, axis, route)  13.6 us
    ppermute x6, starting transfers between devices, extended(): lax.ppermute(lax.slice_in_dim(block, 0, width, axis=dim), axis, backward)  11.1 us
  transfers between devices with their start and end apart: 24, of which 15 were waited for; matrix products, arithmetic and copies ran while one was open for 6% of the time, Pallas kernels for 0%

commit v1 on v0

--- a/solution.py
+++ b/solution.py
@@ -135,7 +135,7 @@
         change = current - previous
         growth = descent - prev_descent
         change_sq, change_growth = lax.psum(
-            (jnp.sum(change * change), jnp.sum(change * growth)), ("gy", "gx")
+            lax.psum((jnp.sum(change * change), jnp.sum(change * growth)), "gy"), "gx"
         )
         step_size = change_sq / change_growth
         previous, prev_descent = (current, descent)

time: 400 us -> 368 us (0.920)
  blocking collectives: 222 us -> 191 us
    psum x2 -> x4, blocking collectives: 222 us -> 191 us  [the longest x2 141 us: per_device(): lax.psum(lax.psum((jnp.sum(change * change), jnp.sum(change * growth)), '...]
where the time goes in v1:
time: 368 us; the launch traced here: 366 us
  blocking collectives  191 us (52%)
  starting transfers between devices  64.1 us (17%)
  local copies, waits for them, and re-layouts  40.2 us (11%)
  waiting for transfers between devices  35.9 us (10%)
  other arithmetic  20.6 us (6%)
  matrix products  11.2 us (3%)
    psum x2, blocking collectives, per_device(): lax.psum(lax.psum((jnp.sum(change * change), jnp.sum(change * growth)), '...  141 us
    psum x2, blocking collectives, per_device(): lax.psum((jnp.sum(change * change), jnp.sum(change * growth)), 'gy')  49.4 us
    ppermute x12, starting transfers between devices, from_behind(): return lax.ppermute(block, axis, route)  28.2 us
    scatter-add x6, local copies, waits for them, and re-layouts, slope_at(): middle.at[:, :, :radius].add(from_left).at[:, :, breadth - radius:]  27.7 us
    ppermute x6, starting transfers between devices, extended(): lax.ppermute(lax.slice_in_dim(block, block.shape[dim] - width, None, axis...  24.2 us
    ppermute x6, waiting for transfers between devices, extended(): lax.ppermute(lax.slice_in_dim(block, 0, width, axis=dim), axis, backward)  17.7 us
    ppermute x12, waiting for transfers between devices, from_behind(): return lax.ppermute(block, axis, route)  14.2 us
    ppermute x6, starting transfers between devices, extended(): lax.ppermute(lax.slice_in_dim(block, 0, width, axis=dim), axis, backward)  11.8 us
  transfers between devices with their start and end apart: 24, of which 15 were waited for; matrix products, arithmetic and copies ran while one was open for 6% of the time, Pallas kernels for 0%

profile of v1, /device:TPU:1, one launch (start us, length us, event | category | flops | bytes accessed | tf_op | source)
XLA Modules:
  0.0 366.4 jit_solution(15697056504585139599)
XLA Ops:
  0.9 4.4 %collective-permute-start = (f32[16,4,128]{2,1,0:T(4,128)S(1)}, f32[16,4,128]{2,1,0:T(4,128)S(1)}, u32[]{:S(2)}, u32[]{:S(2)}) collective-permute-start(f32[16,4,128]{2,1,0:T(4,128)S(1)} %get-tuple-element.213), channel_id=1, source_target_pairs={{0,32},{32,64},{64,96},{96,128},{128,160},{160,192},{192,224},{224... | collective-permute-start | bytes 98312 | tf_op jit(solution)/shard_map/ppermute | solution.py:19
  10.3 5.0 %collective-permute-start.2 = (f32[16,40,4]{2,1,0:T(8,128)S(1)}, f32[16,40,4]{2,1,0:T(8,128)S(1)}, u32[]{:S(2)}, u32[]{:S(2)}) collective-permute-start(f32[16,40,4]{2,1,0:T(8,128)S(1)} %get-tuple-element.207), channel_id=1, source_target_pairs={{0,1},{1,2},{2,3},{3,4},{4,5},{5,6},{6,7},{7,8},{8,9},{9,10},{10,1... | collective-permute-start | bytes 30728 | tf_op jit(solution)/shard_map/ppermute | solution.py:19
  20.3 3.6 collective-permute-done.3
  36.4 3.6 scatter-add.40
  42.1 5.7 %scatter-add.41 = f32[16,40,128]{2,1,0:T(8,128)S(1)} dynamic-update-slice(f32[16,40,128]{2,1,0:T(8,128)S(1)} %scatter-add.40, f32[16,40,4]{2,1,0:T(8,128)} %slice_add_fusion.2, s32[]{:T(128)} %constant.298.clone.1, s32[]{:T(128)} %constant.298.clone.1, s32[]{:T(128)} %constant.301.clone.1) | dynamic-update-slice | bytes 20484 | tf_op jit(solution)/shard_map/scatter-add | solution.py:116
  47.9 3.5 collective-permute-start.6
  53.2 4.6 %collective-permute-done.7 = f32[16,4,128]{2,1,0:T(4,128)S(1)} collective-permute-done((f32[16,4,128]{2,1,0:T(4,128)S(1)}, f32[16,4,128]{2,1,0:T(4,128)S(1)}, u32[]{:S(2)}, u32[]{:S(2)}) %collective-permute-start.7) | collective-permute-done | bytes 32800 | tf_op jit(solution)/shard_map/ppermute | solution.py:30
  59.0 4.8 %collective-permute-start.8 = (f32[16,4,128]{2,1,0:T(4,128)S(1)}, f32[16,4,128]{2,1,0:T(4,128)S(1)}, u32[]{:S(2)}, u32[]{:S(2)}) collective-permute-start(f32[16,4,128]{2,1,0:T(4,128)S(1)} %get-tuple-element.211), channel_id=1, source_target_pairs={{0,32},{32,64},{64,96},{96,128},{128,160},{160,192},{192,224},{224... | collective-permute-start | bytes 98312 | tf_op jit(solution)/shard_map/ppermute | solution.py:19
  68.7 6.7 %collective-permute-start.10 = (f32[16,40,4]{2,1,0:T(8,128)S(1)}, f32[16,40,4]{2,1,0:T(8,128)S(1)}, u32[]{:S(2)}, u32[]{:S(2)}) collective-permute-start(f32[16,40,4]{2,1,0:T(8,128)S(1)} %get-tuple-element.203), channel_id=1, source_target_pairs={{0,1},{1,2},{2,3},{3,4},{4,5},{5,6},{6,7},{7,8},{8,9},{9,10},{10,1... | collective-permute-start | bytes 30728 | tf_op jit(solution)/shard_map/ppermute | solution.py:19
  80.4 3.4 collective-permute-done.11
  97.6 3.5 scatter-add.46
  102.6 5.7 %scatter-add.49 = f32[16,40,128]{2,1,0:T(8,128)S(1)} dynamic-update-slice(f32[16,40,128]{2,1,0:T(8,128)S(1)} %scatter-add.46, f32[16,40,4]{2,1,0:T(8,128)S(1)} %slice_add_fusion.1, s32[]{:T(128)} %constant.298.clone.1, s32[]{:T(128)} %constant.298.clone.1, s32[]{:T(128)} %constant.301.clone.1) | dynamic-update-slice | bytes 20484 | tf_op jit(solution)/shard_map/scatter-add | solution.py:116
  108.3 4.1 %collective-permute-start.14 = (f32[16,4,128]{2,1,0:T(4,128)S(1)}, f32[16,4,128]{2,1,0:T(4,128)S(1)}, u32[]{:S(2)}, u32[]{:S(2)}) collective-permute-start(f32[16,4,128]{2,1,0:T(4,128)S(1)} %get-tuple-element.202), channel_id=1, source_target_pairs={{0,32},{32,64},{64,96},{96,128},{128,160},{160,192},{192,224},{224... | collective-permute-start | bytes 98312 | tf_op jit(solution)/shard_map/ppermute | solution.py:30
  114.4 3.6 collective-permute-done.15
  119.1 25.6 %all-reduce.9 = (f32[]{:T(128)}, f32[]{:T(128)}) all-reduce(f32[]{:T(128)} %get-tuple-element.152, f32[]{:T(128)} %get-tuple-element.151), channel_id=1, replica_groups=mesh['gy'=16,'gx'=32] {'gy'}, use_global_device_ids=true, to_apply=%region_9.10 | all-reduce | flops 2 | bytes 16 | tf_op jit(solution)/shard_map/psum | solution.py:138
  144.7 71.1 %all-reduce.7 = (f32[]{:T(128)}, f32[]{:T(128)}) all-reduce(f32[]{:T(128)} %get-tuple-element.164, f32[]{:T(128)} %get-tuple-element.165), channel_id=1, replica_groups=mesh['gy'=16,'gx'=32] {'gx'}, use_global_device_ids=true, to_apply=%region_10.11 | all-reduce | flops 2 | bytes 16 | tf_op jit(solution)/shard_map/psum | solution.py:137
  219.7 3.6 collective-permute-done.17
  230.4 3.4 collective-permute-done.19
  248.2 3.6 scatter-add.54
  253.6 5.7 %scatter-add.55 = f32[16,40,128]{2,1,0:T(8,128)S(1)} dynamic-update-slice(f32[16,40,128]{2,1,0:T(8,128)S(1)} %scatter-add.54, f32[16,40,4]{2,1,0:T(8,128)} %slice_add_fusion, s32[]{:T(128)} %constant.298.clone.1, s32[]{:T(128)} %constant.298.clone.1, s32[]{:T(128)} %constant.301.clone.1) | dynamic-update-slice | bytes 20484 | tf_op jit(solution)/shard_map/scatter-add | solution.py:116
  259.4 3.4 collective-permute-start.22
  264.7 4.6 %collective-permute-done.23 = f32[16,4,128]{2,1,0:T(4,128)S(1)} collective-permute-done((f32[16,4,128]{2,1,0:T(4,128)S(1)}, f32[16,4,128]{2,1,0:T(4,128)S(1)}, u32[]{:S(2)}, u32[]{:S(2)}) %collective-permute-start.23) | collective-permute-done | bytes 32800 | tf_op jit(solution)/shard_map/ppermute | solution.py:30
  270.4 23.8 %all-reduce.8 = (f32[]{:T(128)}, f32[]{:T(128)}) all-reduce(f32[]{:T(128)} %get-tuple-element.150, f32[]{:T(128)} %get-tuple-element.149), channel_id=1, replica_groups=mesh['gy'=16,'gx'=32] {'gy'}, use_global_device_ids=true, to_apply=%region_15.16 | all-reduce | flops 2 | bytes 16 | tf_op jit(solution)/shard_map/psum | solution.py:138
  294.2 70.3 %all-reduce.6 = (f32[]{:T(128)}, f32[]{:T(128)}) all-reduce(f32[]{:T(128)} %get-tuple-element.162, f32[]{:T(128)} %get-tuple-element.163), channel_id=1, replica_groups=mesh['gy'=16,'gx'=32] {'gx'}, use_global_device_ids=true, to_apply=%region_16.17 | all-reduce | flops 2 | bytes 16 | tf_op jit(solution)/shard_map/psum | solution.py:137
  (213 shorter events, 85.5 us)
Async XLA Ops:
  0.9 8.8 %collective-permute-start = (f32[16,4,128]{2,1,0:T(4,128)S(1)}, f32[16,4,128]{2,1,0:T(4,128)S(1)}, u32[]{:S(2)}, u32[]{:S(2)}) collective-permute-start(f32[16,4,128]{2,1,0:T(4,128)S(1)} %get-tuple-element.213), channel_id=1, source_target_pairs={{0,32},{32,64},{64,96},{96,128},{128,160},{160,192},{192,224},{224... | collective-permute-start | bytes 98312 | tf_op jit(solution)/shard_map/ppermute | solution.py:19
  5.3 4.8 %collective-permute-start.1 = (f32[16,4,128]{2,1,0:T(4,128)S(1)}, f32[16,4,128]{2,1,0:T(4,128)S(1)}, u32[]{:S(2)}, u32[]{:S(2)}) collective-permute-start(f32[16,4,128]{2,1,0:T(4,128)S(1)} %get-tuple-element.214), channel_id=1, source_target_pairs={{32,0},{64,32},{96,64},{128,96},{160,128},{192,160},{224,192},{256... | collective-permute-start | bytes 98312 | tf_op jit(solution)/shard_map/ppermute | solution.py:22
  10.3 9.0 %collective-permute-start.2 = (f32[16,40,4]{2,1,0:T(8,128)S(1)}, f32[16,40,4]{2,1,0:T(8,128)S(1)}, u32[]{:S(2)}, u32[]{:S(2)}) collective-permute-start(f32[16,40,4]{2,1,0:T(8,128)S(1)} %get-tuple-element.207), channel_id=1, source_target_pairs={{0,1},{1,2},{2,3},{3,4},{4,5},{5,6},{6,7},{7,8},{8,9},{9,10},{10,1... | collective-permute-start | bytes 30728 | tf_op jit(solution)/shard_map/ppermute | solution.py:19
  15.4 8.4 %collective-permute-start.3 = (f32[16,40,4]{2,1,0:T(8,128)S(1)}, f32[16,40,4]{2,1,0:T(8,128)S(1)}, u32[]{:S(2)}, u32[]{:S(2)}) collective-permute-start(f32[16,40,4]{2,1,0:T(8,128)S(1)} %get-tuple-element.208), channel_id=1, source_target_pairs={{1,0},{2,1},{3,2},{4,3},{5,4},{6,5},{7,6},{8,7},{9,8},{10,9},{11,1... | collective-permute-start | bytes 30728 | tf_op jit(solution)/shard_map/ppermute | solution.py:22
  29.6 5.9 %collective-permute-start.4 = (f32[16,40,4]{2,1,0:T(8,128)S(1)}, f32[16,40,4]{2,1,0:T(8,128)S(1)}, u32[]{:S(2)}, u32[]{:S(2)}) collective-permute-start(f32[16,40,4]{2,1,0:T(8,128)S(1)} %copy.86), channel_id=1, source_target_pairs={{0,1},{1,2},{2,3},{3,4},{4,5},{5,6},{6,7},{7,8},{8,9},{9,10},{10,1... | collective-permute-start | bytes 30728 | tf_op jit(solution)/shard_map/ppermute | solution.py:30
  31.6 8.7 %collective-permute-start.5 = (f32[16,40,4]{2,1,0:T(8,128)}, f32[16,40,4]{2,1,0:T(8,128)}, u32[]{:S(2)}, u32[]{:S(2)}) collective-permute-start(f32[16,40,4]{2,1,0:T(8,128)} %copy.87), channel_id=1, source_target_pairs={{1,0},{2,1},{3,2},{4,3},{5,4},{6,5},{7,6},{8,7},{9,8},{10,9},{11,1... | collective-permute-start | bytes 30728 | tf_op jit(solution)/shard_map/ppermute | solution.py:30
  47.9 5.3 %collective-permute-start.6 = (f32[16,4,128]{2,1,0:T(4,128)S(1)}, f32[16,4,128]{2,1,0:T(4,128)S(1)}, u32[]{:S(2)}, u32[]{:S(2)}) collective-permute-start(f32[16,4,128]{2,1,0:T(4,128)S(1)} %get-tuple-element.206), channel_id=1, source_target_pairs={{0,32},{32,64},{64,96},{96,128},{128,160},{160,192},{192,224},{224... | collective-permute-start | bytes 98312 | tf_op jit(solution)/shard_map/ppermute | solution.py:30
  51.9 6.0 %collective-permute-start.7 = (f32[16,4,128]{2,1,0:T(4,128)S(1)}, f32[16,4,128]{2,1,0:T(4,128)S(1)}, u32[]{:S(2)}, u32[]{:S(2)}) collective-permute-start(f32[16,4,128]{2,1,0:T(4,128)S(1)} %get-tuple-element.205), channel_id=1, source_target_pairs={{32,0},{64,32},{96,64},{128,96},{160,128},{192,160},{224,192},{256... | collective-permute-start | bytes 98312 | tf_op jit(solution)/shard_map/ppermute | solution.py:30
  59.0 6.2 %collective-permute-start.8 = (f32[16,4,128]{2,1,0:T(4,128)S(1)}, f32[16,4,128]{2,1,0:T(4,128)S(1)}, u32[]{:S(2)}, u32[]{:S(2)}) collective-permute-start(f32[16,4,128]{2,1,0:T(4,128)S(1)} %get-tuple-element.211), channel_id=1, source_target_pairs={{0,32},{32,64},{64,96},{96,128},{128,160},{160,192},{192,224},{224... | collective-permute-start | bytes 98312 | tf_op jit(solution)/shard_map/ppermute | solution.py:19
  63.9 4.7 %collective-permute-start.9 = (f32[16,4,128]{2,1,0:T(4,128)S(1)}, f32[16,4,128]{2,1,0:T(4,128)S(1)}, u32[]{:S(2)}, u32[]{:S(2)}) collective-permute-start(f32[16,4,128]{2,1,0:T(4,128)S(1)} %get-tuple-element.212), channel_id=1, source_target_pairs={{32,0},{64,32},{96,64},{128,96},{160,128},{192,160},{224,192},{256... | collective-permute-start | bytes 98312 | tf_op jit(solution)/shard_map/ppermute | solution.py:22
  68.7 10.7 %collective-permute-start.10 = (f32[16,40,4]{2,1,0:T(8,128)S(1)}, f32[16,40,4]{2,1,0:T(8,128)S(1)}, u32[]{:S(2)}, u32[]{:S(2)}) collective-permute-start(f32[16,40,4]{2,1,0:T(8,128)S(1)} %get-tuple-element.203), channel_id=1, source_target_pairs={{0,1},{1,2},{2,3},{3,4},{4,5},{5,6},{6,7},{7,8},{8,9},{9,10},{10,1... | collective-permute-start | bytes 30728 | tf_op jit(solution)/shard_map/ppermute | solution.py:19
  75.5 8.4 %collective-permute-start.11 = (f32[16,40,4]{2,1,0:T(8,128)S(1)}, f32[16,40,4]{2,1,0:T(8,128)S(1)}, u32[]{:S(2)}, u32[]{:S(2)}) collective-permute-start(f32[16,40,4]{2,1,0:T(8,128)S(1)} %get-tuple-element.204), channel_id=1, source_target_pairs={{1,0},{2,1},{3,2},{4,3},{5,4},{6,5},{7,6},{8,7},{9,8},{10,9},{11,1... | collective-permute-start | bytes 30728 | tf_op jit(solution)/shard_map/ppermute | solution.py:22
  90.7 6.7 %collective-permute-start.12 = (f32[16,40,4]{2,1,0:T(8,128)S(1)}, f32[16,40,4]{2,1,0:T(8,128)S(1)}, u32[]{:S(2)}, u32[]{:S(2)}) collective-permute-start(f32[16,40,4]{2,1,0:T(8,128)S(1)} %copy.90), channel_id=1, source_target_pairs={{0,1},{1,2},{2,3},{3,4},{4,5},{5,6},{6,7},{7,8},{8,9},{9,10},{10,1... | collective-permute-start | bytes 30728 | tf_op jit(solution)/shard_map/ppermute | solution.py:30
  92.7 8.8 %collective-permute-start.13 = (f32[16,40,4]{2,1,0:T(8,128)}, f32[16,40,4]{2,1,0:T(8,128)}, u32[]{:S(2)}, u32[]{:S(2)}) collective-permute-start(f32[16,40,4]{2,1,0:T(8,128)} %copy.91), channel_id=1, source_target_pairs={{1,0},{2,1},{3,2},{4,3},{5,4},{6,5},{7,6},{8,7},{9,8},{10,9},{11,1... | collective-permute-start | bytes 30728 | tf_op jit(solution)/shard_map/ppermute | solution.py:30
  108.3 6.0 %collective-permute-start.14 = (f32[16,4,128]{2,1,0:T(4,128)S(1)}, f32[16,4,128]{2,1,0:T(4,128)S(1)}, u32[]{:S(2)}, u32[]{:S(2)}) collective-permute-start(f32[16,4,128]{2,1,0:T(4,128)S(1)} %get-tuple-element.202), channel_id=1, source_target_pairs={{0,32},{32,64},{64,96},{96,128},{128,160},{160,192},{192,224},{224... | collective-permute-start | bytes 98312 | tf_op jit(solution)/shard_map/ppermute | solution.py:30
  112.9 5.1 %collective-permute-start.15 = (f32[16,4,128]{2,1,0:T(4,128)S(1)}, f32[16,4,128]{2,1,0:T(4,128)S(1)}, u32[]{:S(2)}, u32[]{:S(2)}) collective-permute-start(f32[16,4,128]{2,1,0:T(4,128)S(1)} %get-tuple-element.201), channel_id=1, source_target_pairs={{32,0},{64,32},{96,64},{128,96},{160,128},{192,160},{224,192},{256... | collective-permute-start | bytes 98312 | tf_op jit(solution)/shard_map/ppermute | solution.py:30
  217.1 2.6 collective-permute-start.16
  218.4 4.9 %collective-permute-start.17 = (f32[16,4,128]{2,1,0:T(4,128)S(1)}, f32[16,4,128]{2,1,0:T(4,128)S(1)}, u32[]{:S(2)}, u32[]{:S(2)}) collective-permute-start(f32[16,4,128]{2,1,0:T(4,128)S(1)} %get-tuple-element.210), channel_id=1, source_target_pairs={{32,0},{64,32},{96,64},{128,96},{160,128},{192,160},{224,192},{256... | collective-permute-start | bytes 98312 | tf_op jit(solution)/shard_map/ppermute | solution.py:22
  223.5 5.9 %collective-permute-start.18 = (f32[16,40,4]{2,1,0:T(8,128)S(1)}, f32[16,40,4]{2,1,0:T(8,128)S(1)}, u32[]{:S(2)}, u32[]{:S(2)}) collective-permute-start(f32[16,40,4]{2,1,0:T(8,128)S(1)} %get-tuple-element.199), channel_id=1, source_target_pairs={{0,1},{1,2},{2,3},{3,4},{4,5},{5,6},{6,7},{7,8},{8,9},{9,10},{10,1... | collective-permute-start | bytes 30728 | tf_op jit(solution)/shard_map/ppermute | solution.py:19
  225.4 8.4 %collective-permute-start.19 = (f32[16,40,4]{2,1,0:T(8,128)S(1)}, f32[16,40,4]{2,1,0:T(8,128)S(1)}, u32[]{:S(2)}, u32[]{:S(2)}) collective-permute-start(f32[16,40,4]{2,1,0:T(8,128)S(1)} %get-tuple-element.200), channel_id=1, source_target_pairs={{1,0},{2,1},{3,2},{4,3},{5,4},{6,5},{7,6},{8,7},{9,8},{10,9},{11,1... | collective-permute-start | bytes 30728 | tf_op jit(solution)/shard_map/ppermute | solution.py:22
  240.6 6.7 %collective-permute-start.20 = (f32[16,40,4]{2,1,0:T(8,128)S(1)}, f32[16,40,4]{2,1,0:T(8,128)S(1)}, u32[]{:S(2)}, u32[]{:S(2)}) collective-permute-start(f32[16,40,4]{2,1,0:T(8,128)S(1)} %copy.94), channel_id=1, source_target_pairs={{0,1},{1,2},{2,3},{3,4},{4,5},{5,6},{6,7},{7,8},{8,9},{9,10},{10,1... | collective-permute-start | bytes 30728 | tf_op jit(solution)/shard_map/ppermute | solution.py:30
  242.5 9.2 %collective-permute-start.21 = (f32[16,40,4]{2,1,0:T(8,128)}, f32[16,40,4]{2,1,0:T(8,128)}, u32[]{:S(2)}, u32[]{:S(2)}) collective-permute-start(f32[16,40,4]{2,1,0:T(8,128)} %copy.95), channel_id=1, source_target_pairs={{1,0},{2,1},{3,2},{4,3},{5,4},{6,5},{7,6},{8,7},{9,8},{10,9},{11,1... | collective-permute-start | bytes 30728 | tf_op jit(solution)/shard_map/ppermute | solution.py:30
  259.4 5.3 %collective-permute-start.22 = (f32[16,4,128]{2,1,0:T(4,128)S(1)}, f32[16,4,128]{2,1,0:T(4,128)S(1)}, u32[]{:S(2)}, u32[]{:S(2)}) collective-permute-start(f32[16,4,128]{2,1,0:T(4,128)S(1)} %get-tuple-element.198), channel_id=1, source_target_pairs={{0,32},{32,64},{64,96},{96,128},{128,160},{160,192},{192,224},{224... | collective-permute-start | bytes 98312 | tf_op jit(solution)/shard_map/ppermute | solution.py:30
  263.2 6.1 %collective-permute-start.23 = (f32[16,4,128]{2,1,0:T(4,128)S(1)}, f32[16,4,128]{2,1,0:T(4,128)S(1)}, u32[]{:S(2)}, u32[]{:S(2)}) collective-permute-start(f32[16,4,128]{2,1,0:T(4,128)S(1)} %get-tuple-element.197), channel_id=1, source_target_pairs={{32,0},{64,32},{96,64},{128,96},{160,128},{192,160},{224,192},{256... | collective-permute-start | bytes 98312 | tf_op jit(solution)/shard_map/ppermute | solution.py:30
  (34 other events, 339.8 us)
